TPU v7x, 32 devices: a whole 2x2x4 slice. The times are simulated.
32 devices in a mesh: groups: 2 (over x), tok: 16 (over z, y, core).
Axes of the slice: x: 2, y: 2, z: 4, core: 2. Of those that a mesh axis runs over, the one named last changes fastest.
Arguments:
- queries: bfloat16 [4096, 4096], P(('groups', 'tok')), parts along dimension 0, may hold values from -8 to 8
- new_keys: bfloat16 [4096, 512], P(('groups', 'tok')), parts along dimension 0, may hold values from -8 to 8
- new_values: bfloat16 [4096, 512], P(('groups', 'tok')), parts along dimension 0, may hold values from -6 to 6
- cache_keys: bfloat16 [65536, 512], P(('groups', 'tok')), parts along dimension 0, may hold values from -8 to 8
- cache_values: bfloat16 [65536, 512], P(('groups', 'tok')), parts along dimension 0, may hold values from -6 to 6
- cache_lens: int32 [32], P(('groups', 'tok')), parts along dimension 0, may hold values from 1 to 2048, 20480 in all
- residual: bfloat16 [4096, 2048], P(('groups', 'tok')), parts along dimension 0, may hold values from -40 to 40
- out_weight: bfloat16 [4096, 2048], P('tok'), may hold values from -0.09375 to 0.09375
- norm_gain: float32 [2048], replicated, may hold values from 0.25 to 1.75
- expert_ids: int32 [4096, 8], P(('groups', 'tok')), parts along dimension 0, may hold values from 0 to 63, all different within a row; in each aligned block of 64 rows (0 to 63, 64 to 127, ...) at most 12 rows name the same one
- route_weights: float32 [4096, 8], P(('groups', 'tok')), parts along dimension 0, may hold values from 0.2 to 1
- gate_weight: bfloat16 [64, 2048, 384], P('tok'), may hold values from -0.125 to 0.125
- up_weight: bfloat16 [64, 2048, 384], P('tok'), may hold values from -0.125 to 0.125
- down_weight: bfloat16 [64, 384, 2048], P('tok'), may hold values from -0.3125 to 0.3125
Outputs:
- layer_out: bfloat16 [4096, 2048], P(('groups', 'tok')), parts along dimension 0
There are 2 independent parts, one for each index of `groups`. A program takes and returns all parts, laid end to end along the dimension named above; an argument that names none is the same for every part. Nothing has to cross between parts.
Inputs may be any that keep to these rules, and one draw needn't show every extreme that they name: `expert_ids`: each row names 8 different experts. In each aligned block of 64 rows no expert is named by more than 12 rows; that many is reached in some block. `cache_lens`: the largest length equals 2048.
All inputs are finite; a program needn't handle non-finite values. No bound on the sum of `cache_lens` on one device may be relied on, other than what follows from the above.
Results may differ from a plain program's by a relative error of at most 0.009.
Values may be sent and summed in bfloat16 or wider, within the bound.
No kernel may reach another device: no remote copies, remote signals or barrier semaphores. Data moves between devices by JAX's collectives and lax.ppermute only.
A program may use at most 128 MiB of HBM per device.

v0:
```python
import jax
import jax.numpy as jnp
from jax import lax
from jax.sharding import PartitionSpec as P

HEADS = 32
KVH = 4
HD = 128


def head_attention(query_rows, key_rows, value_rows, allowed):

    def one_head(operands):
        query_head, key_head, value_head = operands
        scores = jnp.einsum("rgd,kd->rgk", query_head, key_head, preferred_element_type=jnp.float32)
        scores = scores * query_head.shape[-1] ** (-0.5)
        scores = jnp.where(allowed[:, None, :], scores, -1e30)
        highest = jnp.max(scores, axis=-1, keepdims=True)
        weights = jnp.exp(scores - highest)
        weights = (weights / jnp.sum(weights, axis=-1, keepdims=True)).astype(jnp.bfloat16)
        return jnp.einsum(
            "rgk,kd->rgd", weights, value_head, preferred_element_type=jnp.float32
        ).astype(jnp.bfloat16)

    return lax.map(one_head, (query_rows, key_rows, value_rows))


def body(
    queries,
    new_keys,
    new_values,
    cache_keys,
    cache_values,
    cache_lens,
    residual,
    out_weight,
    norm_gain,
    expert_ids,
    route_weights,
    gate_weight,
    up_weight,
    down_weight,
):
    devices = lax.axis_size("tok")
    group = HEADS // KVH
    row_count = residual.shape[0]
    block_rows = row_count // 2
    top_count = expert_ids.shape[1]
    experts_local = gate_weight.shape[0]
    experts_all = experts_local * devices
    capacity = max(2, block_rows * top_count * 3 // (2 * experts_all))
    cache_rows = cache_keys.shape[0]
    length = cache_lens[0]
    key_all = jnp.concatenate([cache_keys, new_keys], 0).reshape(-1, KVH, HD).transpose(1, 0, 2)
    value_all = (
        jnp.concatenate([cache_values, new_values], 0).reshape(-1, KVH, HD).transpose(1, 0, 2)
    )
    full_weight = lax.all_gather(out_weight, "tok", axis=0, tiled=True)
    pieces = []
    for half in range(2):
        lower = half * block_rows
        upper = lower + block_rows
        query_block = queries[lower:upper]
        count_rows = query_block.shape[0]
        positions = lower + jnp.arange(count_rows)
        cache_ok = jnp.broadcast_to(
            jnp.arange(cache_rows)[None, :] < length, (count_rows, cache_rows)
        )
        new_ok = jnp.arange(new_keys.shape[0])[None, :] <= positions[:, None]
        allowed = jnp.concatenate([cache_ok, new_ok], 1)
        shaped = query_block.reshape(count_rows, KVH, group, HD).transpose(1, 0, 2, 3)
        output = head_attention(shaped, key_all, value_all, allowed)
        attended = output.transpose(1, 0, 2, 3).reshape(count_rows, HEADS * HD)
        mixed = residual[lower:upper].astype(jnp.float32) + jnp.dot(
            attended, full_weight, preferred_element_type=jnp.float32
        )
        factor = lax.rsqrt(jnp.mean(mixed * mixed, axis=-1, keepdims=True) + 1e-06)
        finish_normed = (mixed * factor * norm_gain).astype(jnp.bfloat16)
        mixed, normed = (mixed, finish_normed)
        blocks = normed.shape[0] // block_rows
        flat_ids = expert_ids[lower:upper].reshape(blocks, block_rows * top_count)
        matches = (flat_ids[:, :, None] == jnp.arange(experts_all)[None, None, :]).astype(jnp.int32)
        ranking = jnp.sum(jnp.cumsum(matches, axis=1) * matches, axis=-1) - 1
        owner_device = flat_ids // experts_local
        local_expert = flat_ids % experts_local
        block_index = jnp.arange(blocks)[:, None]
        slot_index = (
            ((local_expert * devices + owner_device) * blocks + block_index) * capacity + ranking
        ).reshape(-1)
        token_index = (
            block_index * block_rows + jnp.arange(block_rows * top_count)[None, :] // top_count
        ).reshape(-1)
        total_slots = experts_local * devices * blocks * capacity
        source_row = jnp.zeros((total_slots,), jnp.int32).at[slot_index].set(token_index)
        filled = jnp.zeros((total_slots,), jnp.bool_).at[slot_index].set(True)
        outgoing = jnp.where(filled[:, None], normed[source_row], jnp.zeros((), jnp.bfloat16))
        outgoing = outgoing.reshape(experts_local, devices, blocks * capacity, -1)
        arrived = lax.all_to_all(outgoing, "tok", split_axis=1, concat_axis=1, tiled=True)
        slot_count = arrived.shape[2]
        stacked = arrived.reshape(experts_local, devices * slot_count, -1)
        gate_part = jnp.einsum(
            "erd,edf->erf", stacked, gate_weight, preferred_element_type=jnp.float32
        )
        up_part = jnp.einsum("erd,edf->erf", stacked, up_weight, preferred_element_type=jnp.float32)
        hidden = (jax.nn.silu(gate_part) * up_part).astype(jnp.bfloat16)
        result = jnp.einsum(
            "erf,efd->erd", hidden, down_weight, preferred_element_type=jnp.float32
        ).astype(jnp.bfloat16)
        result = result.reshape(experts_local, devices, slot_count, -1)
        returned = lax.all_to_all(result, "tok", split_axis=1, concat_axis=1, tiled=True)
        picked = returned.reshape(total_slots, -1)[slot_index].astype(jnp.float32)
        picked = (
            picked.reshape(-1, top_count, picked.shape[-1]) * route_weights[lower:upper][:, :, None]
        )
        pieces.append(mixed + jnp.sum(picked, axis=1))
    final = jnp.concatenate(pieces, 0)
    return final.astype(jnp.bfloat16)


def solution(mesh):
    placed = (
        P(("groups", "tok"), None),
        P(("groups", "tok"), None),
        P(("groups", "tok"), None),
        P(("groups", "tok"), None),
        P(("groups", "tok"), None),
        P(("groups", "tok")),
        P(("groups", "tok"), None),
        P("tok", None),
        P(),
        P(("groups", "tok"), None),
        P(("groups", "tok"), None),
        P("tok", None, None),
        P("tok", None, None),
        P("tok", None, None),
    )
    return jax.shard_map(
        body, mesh=mesh, in_specs=placed, out_specs=P(("groups", "tok"), None), check_vma=False
    )
```

profile of v0, /device:TPU:13, one launch (start us, length us, event | category | flops | bytes accessed | tf_op | source)
XLA Modules:
  0.0 497.2 jit_solution(4456463768971965499)
XLA Ops:
  30.3 30.9 %while.20 = (s32[]{:T(128)}, bf16[4,64,8,128]{3,2,1,0:T(8,128)(2,1)S(1)}, pred[64,2176]{1,0:T(8,128)(4,1)S(1)}, bf16[4,64,8,128]{3,2,0,1:T(8,128)(2,1)S(1)}, bf1...) while((s32[]{:T(128)}, bf16[4,64,8,128]{3,2,1,0:T(8,128)(2,1)S(1)}, ...), condition=%wide.region_3.4_spmd, body=%wide.region_0.3_spmd.sunk | while | flops 577177728 | bytes 10465357 | solution.py:25
  30.3 4.5 fusion.146
  38.1 4.5 fusion.146
  45.8 4.5 fusion.146
  53.5 4.5 fusion.146
  63.4 32.3 %while.21 = (s32[]{:T(128)}, bf16[4,64,8,128]{3,2,1,0:T(8,128)(2,1)S(1)}, pred[64,2176]{1,0:T(8,128)(4,1)S(1)}, bf16[4,64,8,128]{3,2,0,1:T(8,128)(2,1)}, bf16[4,...) while((s32[]{:T(128)}, bf16[4,64,8,128]{3,2,1,0:T(8,128)(2,1)S(1)}, ...), condition=%wide.region_14.15_spmd, body=%wide.region_11.14_spmd.sunk | while | flops 577177728 | bytes 10465357 | solution.py:25
  63.4 4.8 fusion.151
  71.6 4.8 fusion.151
  79.6 4.8 fusion.151
  87.7 4.8 fusion.151
  103.3 31.6 %all-gather.2.cloned.1.call-done = bf16[4096,2048]{1,0:T(8,128)(2,1)} async-done(((bf16[256,2048]{1,0:T(8,128)(2,1)}), bf16[4096,2048]{1,0:T(8,128)(2,1)}) %all-gather.2.cloned.1.call-update) | async-done | bytes 16777232 | tf_op jit(solution)/shard_map/all_gather | solution.py:58
  134.9 9.1 %multiply_reduce_fusion.1 = (f32[64]{0:T(128)S(1)}, f32[64,2048]{1,0:T(8,128)S(1)}) fusion(bf16[4096,2048]{1,0:T(8,128)(2,1)} %all-gather.2.cloned.1.call-done, bf16[8,8,32,128]{3,2,1,0:T(8,128)(2,1)S(1)} %bitcast.164, bf16[128,2048]{1,0:T(8,128)(2,1)} %param.24), kind=kOutput, calls=%fused_computation.95 | convolution fusion | flops 1074266112 | bytes 18088192 | tf_op jit(solution)/shard_map/dot_general | solution.py:74
  154.1 6.1 %gather.17 = bf16[4,16,12,2048]{3,2,1,0:T(8,128)(2,1)} reshape(bf16[768,2048]{1,0:T(8,128)(2,1)} %gather_fusion) | data formatting | bytes 6291456 | tf_op jit(solution)/shard_map/gather | solution.py:96
  162.8 4.4 copy.62
  167.1 8.0 %all-to-all-start = ((bf16[4,16,12,2048]{3,0,2,1:T(4,128)(2,1)}), bf16[4,16,12,2048]{3,0,2,1:T(4,128)(2,1)}, u32[]{:S(2)}, u32[]{:S(2)}) async-start(bf16[4,16,12,2048]{3,0,2,1:T(4,128)(2,1)} %copy.62), calls=%async_computation | async-start | bytes 6291456 | tf_op jit(solution)/shard_map/all_to_all | solution.py:98
  191.3 4.4 copy.77
  195.7 49.3 %all-to-all-done = bf16[4,16,12,2048]{3,0,2,1:T(4,128)(2,1)} async-done(((bf16[4,16,12,2048]{3,0,2,1:T(4,128)(2,1)}), bf16[4,16,12,2048]{3,0,2,1:T(4,128)(2,1)}, u32[]{:S(2)}, u32[]{:S(2)}) %all-to-all-start) | async-done | bytes 3145760 | tf_op jit(solution)/shard_map/all_to_all | solution.py:98
  245.0 4.9 all-to-all-start.2
  249.9 9.0 %fusion.70 = f32[4,192,384]{2,1,0:T(8,128)} fusion(bf16[4,2048,384]{2,1,0:T(8,128)(2,1)} %param.29, bf16[4,192,2048]{2,0,1:T(4,128)(2,1)} %bitcast.27), kind=kOutput, calls=%fused_computation.70 | convolution fusion | flops 1207959552 | bytes 10616832 | tf_op jit(solution)/shard_map/erd,edf->erf/dot_general | solution.py:101
  258.8 13.5 %convolution_convert_fusion.1 = bf16[4,192,2048]{2,1,0:T(8,128)(2,1)} fusion(bf16[4,384,2048]{2,1,0:T(8,128)(2,1)} %param.31, bf16[4,2048,384]{2,1,0:T(8,128)(2,1)} %param.30, bf16[4,192,2048]{2,0,1:T(4,128)(2,1)} %bitcast.27, f32[4,192,384]{2,1,0:T(8,128)} %fusion.70), kind=kOutput, calls=%fused_computation.63 | convolution fusion | flops 2419261440 | bytes 20054016 | tf_op jit(solution)/shard_map/erf,efd->erd/dot_general | solution.py:106
  272.4 6.2 %copy.65 = bf16[4,192,2048]{2,0,1:T(4,128)(2,1)} copy(bf16[4,192,2048]{2,1,0:T(8,128)(2,1)} %convolution_convert_fusion.1) | data formatting | bytes 6291456 | tf_op jit(solution)/shard_map/convert_element_type | solution.py:108
  278.6 41.0 %all-to-all-done.2 = bf16[4,16,12,2048]{3,0,2,1:T(4,128)(2,1)S(1)} async-done(((bf16[4,16,12,2048]{3,0,2,1:T(4,128)(2,1)}), bf16[4,16,12,2048]{3,0,2,1:T(4,128)(2,1)S(1)}, u32[]{:S(2)}, u32[]{:S(2)}) %all-to-all-start.2) | async-done | bytes 3145760 | tf_op jit(solution)/shard_map/all_to_all | solution.py:98
  321.3 4.8 all-to-all-start.1
  326.1 9.0 %fusion.66 = f32[4,192,384]{2,1,0:T(8,128)} fusion(bf16[4,2048,384]{2,1,0:T(8,128)(2,1)} %param.29, bf16[4,192,2048]{2,0,1:T(4,128)(2,1)} %bitcast.162), kind=kOutput, calls=%fused_computation.66 | convolution fusion | flops 1207959552 | bytes 10616832 | tf_op jit(solution)/shard_map/erd,edf->erf/dot_general | solution.py:101
  335.1 13.5 %convolution_convert_fusion = bf16[4,192,2048]{2,1,0:T(8,128)(2,1)} fusion(bf16[4,384,2048]{2,1,0:T(8,128)(2,1)} %param.31, bf16[4,2048,384]{2,1,0:T(8,128)(2,1)} %param.30, bf16[4,192,2048]{2,0,1:T(4,128)(2,1)} %bitcast.163, f32[4,192,384]{2,1,0:T(8,128)} %fusion.66), kind=kOutput, calls=%fused_computation.62 | convolution fusion | flops 2419261440 | bytes 20054016 | tf_op jit(solution)/shard_map/erf,efd->erd/dot_general | solution.py:106
  348.6 6.2 %copy.80 = bf16[4,192,2048]{2,0,1:T(4,128)(2,1)} copy(bf16[4,192,2048]{2,1,0:T(8,128)(2,1)} %convolution_convert_fusion) | data formatting | bytes 6291456 | tf_op jit(solution)/shard_map/convert_element_type | solution.py:108
  354.8 41.2 %all-to-all-done.1 = bf16[4,16,12,2048]{3,0,2,1:T(4,128)(2,1)S(1)} async-done(((bf16[4,16,12,2048]{3,0,2,1:T(4,128)(2,1)}), bf16[4,16,12,2048]{3,0,2,1:T(4,128)(2,1)S(1)}, u32[]{:S(2)}, u32[]{:S(2)}) %all-to-all-start.1) | async-done | bytes 3145760 | tf_op jit(solution)/shard_map/all_to_all | solution.py:110
  396.0 4.9 all-to-all-start.3
  404.9 4.7 reshape.750
  417.5 53.4 %all-to-all-done.3 = bf16[4,16,12,2048]{3,0,2,1:T(4,128)(2,1)} async-done(((bf16[4,16,12,2048]{3,0,2,1:T(4,128)(2,1)}), bf16[4,16,12,2048]{3,0,2,1:T(4,128)(2,1)}, u32[]{:S(2)}, u32[]{:S(2)}) %all-to-all-start.3) | async-done | bytes 3145760 | tf_op jit(solution)/shard_map/all_to_all | solution.py:110
  470.9 5.6 %copy.81 = bf16[4,16,12,2048]{3,2,1,0:T(8,128)(2,1)} copy(bf16[4,16,12,2048]{3,0,2,1:T(4,128)(2,1)} %all-to-all-done.3) | data formatting | bytes 6291456 | tf_op jit(solution)/shard_map/all_to_all | solution.py:110
  476.5 4.7 reshape.761
  (121 shorter events, 109.8 us)
Async XLA Ops:
  6.5 8.2 %copy-start.6 = (bf16[128,512]{1,0:T(8,128)(2,1)S(1)}, bf16[128,512]{1,0:T(8,128)(2,1)}, u32[]{:S(2)}) copy-start(bf16[128,512]{1,0:T(8,128)(2,1)} %param.19) | copy-start | bytes 393220
  6.5 128.3 %all-gather.2.cloned.1.call-start = ((), (), s32[]{:S(2)}) async-start(), calls=%async_computation.4 | async-start | bytes 17825792 | tf_op jit(solution)/shard_map/all_gather | solution.py:58
  19.1 4.1 copy-start.7
  27.7 2.6 copy-start.4
  63.4 32.4 %copy-start.8 = (s32[512]{0:T(512)S(1)}, s32[512]{0:T(512)}, u32[]{:S(2)}) copy-start(s32[512]{0:T(512)} %eq.57) | copy-start | bytes 6148
  63.4 34.6 %copy-start.12 = (s32[512,1]{0,1:T(1,128)S(1)}, s32[512,1]{0,1:T(1,128)}, u32[]{:S(2)}) copy-start(s32[512,1]{0,1:T(1,128)} %reshape.742) | copy-start | bytes 6148
  134.9 10.8 %copy-start = (bf16[4096,2048]{1,0:T(8,128)(2,1)S(1)}, bf16[4096,2048]{1,0:T(8,128)(2,1)}, u32[]{:S(2)}) copy-start(bf16[4096,2048]{1,0:T(8,128)(2,1)} %all-gather.2.cloned.1.call-done) | copy-start | bytes 50331652
  134.9 10.8 %copy-start.5 = (bf16[128,2048]{1,0:T(8,128)(2,1)S(1)}, bf16[128,2048]{1,0:T(8,128)(2,1)}, u32[]{:S(2)}) copy-start(bf16[128,2048]{1,0:T(8,128)(2,1)} %param.24) | copy-start | bytes 1572868
  143.9 5.0 %copy-start.2 = (f32[64,2048]{1,0:T(8,128)}, f32[64,2048]{1,0:T(8,128)S(1)}, u32[]{:S(2)}) copy-start(f32[64,2048]{1,0:T(8,128)S(1)} %get-tuple-element.134) | copy-start | bytes 1572868
  145.7 4.0 copy-start.11
  148.9 0.8 copy-start.1
  167.1 8.0 %copy-start.10 = (s32[64,8]{0,1:T(8,128)S(1)}, s32[64,8]{0,1:T(8,128)}, u32[]{:S(2)}) copy-start(s32[64,8]{0,1:T(8,128)} %get-tuple-element.130) | copy-start | bytes 6148
  167.1 77.8 %all-to-all-start = ((bf16[4,16,12,2048]{3,0,2,1:T(4,128)(2,1)}), bf16[4,16,12,2048]{3,0,2,1:T(4,128)(2,1)}, u32[]{:S(2)}, u32[]{:S(2)}) async-start(bf16[4,16,12,2048]{3,0,2,1:T(4,128)(2,1)} %copy.62), calls=%async_computation | async-start | bytes 6291456 | tf_op jit(solution)/shard_map/all_to_all | solution.py:98
  245.0 74.6 %all-to-all-start.2 = ((bf16[4,16,12,2048]{3,0,2,1:T(4,128)(2,1)}), bf16[4,16,12,2048]{3,0,2,1:T(4,128)(2,1)S(1)}, u32[]{:S(2)}, u32[]{:S(2)}) async-start(bf16[4,16,12,2048]{3,0,2,1:T(4,128)(2,1)} %copy.77), calls=%async_computation.2 | async-start | bytes 6291456 | tf_op jit(solution)/shard_map/all_to_all | solution.py:98
  319.6 1.7 copy-start.3
  321.3 74.7 %all-to-all-start.1 = ((bf16[4,16,12,2048]{3,0,2,1:T(4,128)(2,1)}), bf16[4,16,12,2048]{3,0,2,1:T(4,128)(2,1)S(1)}, u32[]{:S(2)}, u32[]{:S(2)}) async-start(bf16[4,16,12,2048]{3,0,2,1:T(4,128)(2,1)} %bitcast.159), calls=%async_computation.1 | async-start | bytes 6291456 | tf_op jit(solution)/shard_map/all_to_all | solution.py:110
  396.0 4.9 copy-start.9
  396.0 74.9 %all-to-all-start.3 = ((bf16[4,16,12,2048]{3,0,2,1:T(4,128)(2,1)}), bf16[4,16,12,2048]{3,0,2,1:T(4,128)(2,1)}, u32[]{:S(2)}, u32[]{:S(2)}) async-start(bf16[4,16,12,2048]{3,0,2,1:T(4,128)(2,1)} %bitcast.158), calls=%async_computation.3 | async-start | bytes 6291456 | tf_op jit(solution)/shard_map/all_to_all | solution.py:110
Sparse Core Ops, SparseCore 0:
  9.5 125.3 all-gather.1
where the time goes:
time: 506 us; the launch traced here: 497 us
  waiting for transfers between devices  217 us (43%)
  matrix products  120 us (24%)
  local copies, waits for them, and re-layouts  99.9 us (20%)
  starting transfers between devices  22.5 us (4%)
  other arithmetic  22.2 us (4%)
  between operations  15 us (3%)
    all_to_all x2, waiting for transfers between devices, body(): lax.all_to_all(result, 'tok', split_axis=1, concat_axis=1, tiled=True)  94.6 us
    all_to_all x2, waiting for transfers between devices, body(): lax.all_to_all(outgoing, 'tok', split_axis=1, concat_axis=1, tiled=True)  90.4 us
    sub x8, matrix products, one_head(): weights = jnp.exp(scores - highest)  37 us
    all_gather x1, waiting for transfers between devices, body(): full_weight = lax.all_gather(out_weight, 'tok', axis=0, tiled=True)  31.6 us
    dot_general x2, matrix products, body(): jnp.einsum('erf,efd->erd', hidden, down_weight, preferred_element_type=jn...  27 us
    dot_general x8, matrix products, one_head(): jnp.einsum('rgk,kd->rgd', weights, value_head, preferred_element_type=jnp...  26 us
    dot_general x2, matrix products, body(): jnp.einsum('erd,edf->erf', stacked, gate_weight, preferred_element_type=j...  17.9 us
    unnamed x33, local copies, waits for them, and re-layouts  16.9 us
  transfers between devices with their start and end apart: 5, of which 5 were waited for; matrix products, arithmetic and copies ran while one was open for 38% of the time, Pallas kernels for 0%

commit v1 on v0

v1 whole, which is shorter than its diff:
```python
import functools
import math

import jax
import jax.numpy as jnp
import numpy as np
from jax import lax
from jax.experimental import pallas as pl
from jax.experimental.pallas import tpu as pltpu
from jax.sharding import PartitionSpec as P

HD = 128
KVH = 4
BLOCK = 64
BF = jnp.bfloat16
F32 = jnp.float32
ANY = pl.BlockSpec(memory_space=pl.ANY)
VMEM_LIMIT = 60 * 1024 * 1024


def attention_piece(lens, queries, new_keys, new_values, cache_keys, cache_values, kv):
    rows = queries.shape[0]
    cache = cache_keys.shape[0]
    width = queries.shape[1] // KVH
    pair = 2 * HD
    scale = HD ** (-0.5) * math.log2(math.e)

    def kernel(lens_ref, q_ref, kn_ref, vn_ref, kc_ref, vc_ref, o_ref, vca_ref, vna_ref, bias_ref):
        @pl.when(pl.program_id(0) == 0)
        def _():
            vca_ref[:, :HD] = vc_ref[...]
            vca_ref[:, HD:] = jnp.ones((cache, HD), BF)
            vna_ref[:, :HD] = vn_ref[...]
            vna_ref[:, HD:] = jnp.ones((rows, HD), BF)
            at = lax.broadcasted_iota(jnp.int32, (8, cache), 1)
            bias_ref[...] = jnp.where(at < lens_ref[0], 0.0, -1e30).astype(F32)

        q = q_ref[...]
        q2 = jnp.concatenate([q[:, :HD], q[:, HD:]], axis=0)
        dims = (((1,), (1,)), ((), ()))
        sc = lax.dot_general(q2, kc_ref[...], dims, preferred_element_type=F32)
        sn = lax.dot_general(q2, kn_ref[...], dims, preferred_element_type=F32)
        sc = sc + bias_ref[0:1, :]
        row = lax.broadcasted_iota(jnp.int32, (2 * rows, rows), 0)
        row = jnp.where(row >= rows, row - rows, row)
        col = lax.broadcasted_iota(jnp.int32, (2 * rows, rows), 1)
        sn = jnp.where(col <= row, sn, -1e30)
        top = jnp.maximum(
            jnp.max(sc, axis=1, keepdims=True), jnp.max(sn, axis=1, keepdims=True)
        )
        pc = jnp.exp2((sc - top) * scale).astype(BF)
        pn = jnp.exp2((sn - top) * scale).astype(BF)
        acc = jnp.dot(pc, vca_ref[...], preferred_element_type=F32)
        acc = acc + jnp.dot(pn, vna_ref[...], preferred_element_type=F32)
        out = (acc[:, :HD] / acc[:, HD:]).astype(BF)
        o_ref[:, :HD] = out[:rows]
        o_ref[:, HD:] = out[rows:]

    steps = width // pair
    keys = cache + rows
    return pl.pallas_call(
        kernel,
        name="attend",
        out_shape=jax.ShapeDtypeStruct((rows, width), BF),
        grid_spec=pltpu.PrefetchScalarGridSpec(
            num_scalar_prefetch=1,
            grid=(steps,),
            in_specs=[
                pl.BlockSpec((rows, pair), lambda i, _: (0, kv * steps + i)),
                pl.BlockSpec((rows, HD), lambda i, _: (0, kv)),
                pl.BlockSpec((rows, HD), lambda i, _: (0, kv)),
                pl.BlockSpec((cache, HD), lambda i, _: (0, kv)),
                pl.BlockSpec((cache, HD), lambda i, _: (0, kv)),
            ],
            out_specs=pl.BlockSpec((rows, pair), lambda i, _: (0, i)),
            scratch_shapes=[
                pltpu.VMEM((cache, 2 * HD), BF),
                pltpu.VMEM((rows, 2 * HD), BF),
                pltpu.VMEM((8, cache), F32),
            ],
        ),
        compiler_params=pltpu.CompilerParams(vmem_limit_bytes=VMEM_LIMIT),
        cost_estimate=pl.CostEstimate(
            flops=4 * rows * width * keys * 2,
            transcendentals=rows * (width // HD) * keys,
            bytes_accessed=4 * keys * HD + 4 * rows * width,
        ),
    )(lens, queries, new_keys, new_values, cache_keys, cache_values)


def project(table, pieces, weights, tail_a, tail_b, half_rows):
    devices = len(pieces)
    rows, width = pieces[0][0].shape
    flat = [p for device in pieces for p in device]
    blocks = len(weights) + 1
    kblock, cols = weights[0].shape
    count = len(flat)

    def kernel(*refs):
        table_ref = refs[0]
        piece_refs = refs[1 : 1 + count]
        weight_refs = refs[1 + count : 1 + count + blocks + 1]
        outs = refs[2 + count + blocks : 2 + count + blocks + devices]
        a_ref, w_ref, a_sem, w_sem = refs[2 + count + blocks + devices :]
        copies = []
        for d in range(devices):
            for j in range(KVH):
                at = d * KVH + j
                copies.append(
                    pltpu.make_async_copy(
                        piece_refs[at],
                        a_ref.at[pl.ds(d * rows, rows), pl.ds(j * width, width)],
                        a_sem.at[at],
                    )
                )
        wcopies = []
        for s in range(blocks - 1):
            wcopies.append(
                [pltpu.make_async_copy(weight_refs[s], w_ref.at[s], w_sem.at[s])]
            )
        wcopies.append(
            [
                pltpu.make_async_copy(
                    weight_refs[blocks - 1],
                    w_ref.at[blocks - 1, pl.ds(0, half_rows)],
                    w_sem.at[blocks - 1],
                ),
                pltpu.make_async_copy(
                    weight_refs[blocks],
                    w_ref.at[blocks - 1, pl.ds(half_rows, half_rows)],
                    w_sem.at[blocks],
                ),
            ]
        )
        for copy in copies:
            copy.start()
        for group in wcopies:
            for copy in group:
                copy.start()
        for copy in copies:
            copy.wait()
        acc = jnp.zeros((devices * rows, cols), F32)
        for s in range(blocks):
            for copy in wcopies[s]:
                copy.wait()
            for half in range(2):
                base = pl.multiple_of(table_ref[2 * s + half], half_rows)
                acc = acc + jnp.dot(
                    a_ref[:, pl.ds(base, half_rows)],
                    w_ref[s, half * half_rows : (half + 1) * half_rows, :],
                    preferred_element_type=F32,
                )
        for d in range(devices):
            outs[d][...] = acc[d * rows : (d + 1) * rows].astype(BF)

    vm = pl.BlockSpec(memory_space=pltpu.VMEM)
    return pl.pallas_call(
        kernel,
        name="project",
        out_shape=[jax.ShapeDtypeStruct((rows, cols), BF)] * devices,
        in_specs=[pl.BlockSpec(memory_space=pltpu.SMEM)] + [ANY] * (count + blocks + 1),
        out_specs=[vm] * devices,
        scratch_shapes=[
            pltpu.VMEM((devices * rows, KVH * width), BF),
            pltpu.VMEM((blocks, kblock, cols), BF),
            pltpu.SemaphoreType.DMA((count,)),
            pltpu.SemaphoreType.DMA((blocks + 1,)),
        ],
        compiler_params=pltpu.CompilerParams(vmem_limit_bytes=VMEM_LIMIT),
        cost_estimate=pl.CostEstimate(
            flops=2 * devices * rows * blocks * kblock * cols,
            transcendentals=0,
            bytes_accessed=2 * (devices * rows * KVH * width + blocks * kblock * cols),
        ),
    )(table, *flat, *weights, tail_a, tail_b)


def mix_norm(table, residual, gain, pieces):
    rows, width = residual.shape
    cols = pieces[0].shape[1]

    def kernel(table_ref, residual_ref, gain_ref, *refs):
        piece_refs = refs[: len(pieces)]
        mixed_ref, normed_ref = refs[len(pieces) :]
        total = jnp.zeros((rows, 1), F32)
        for d in range(len(pieces)):
            at = pl.ds(pl.multiple_of(table_ref[d], cols), cols)
            part = residual_ref[:, at].astype(F32) + piece_refs[d][...].astype(F32)
            mixed_ref[:, at] = part
            total = total + jnp.sum(part * part, axis=1, keepdims=True)
        factor = lax.rsqrt(total / width + 1e-6)
        normed_ref[...] = (mixed_ref[...] * factor * gain_ref[...]).astype(BF)

    vm = pl.BlockSpec(memory_space=pltpu.VMEM)
    return pl.pallas_call(
        kernel,
        name="mixnorm",
        out_shape=[
            jax.ShapeDtypeStruct((rows, width), F32),
            jax.ShapeDtypeStruct((rows, width), BF),
        ],
        in_specs=[pl.BlockSpec(memory_space=pltpu.SMEM)] + [vm] * (2 + len(pieces)),
        out_specs=[vm, vm],
        compiler_params=pltpu.CompilerParams(vmem_limit_bytes=VMEM_LIMIT),
        cost_estimate=pl.CostEstimate(
            flops=6 * rows * width, transcendentals=rows, bytes_accessed=10 * rows * width
        ),
    )(table, residual, gain.reshape(1, -1), *pieces)


def experts(slots, shares, blocks, gate, up, down, capacity):
    local, width, hidden = gate.shape
    sizes = [b.shape[0] for b in blocks]
    starts = [int(v) for v in np.cumsum([0] + sizes)]
    tokens = starts[-1]
    group_blocks = 1
    while group_blocks * capacity % 16 or group_blocks * BLOCK < 256:
        group_blocks *= 2
    span = group_blocks * BLOCK
    per = group_blocks * capacity
    groups = tokens // span
    count = len(blocks)

    def kernel(slots_ref, shares_ref, *refs):
        block_refs = refs[:count]
        gate_ref, up_ref, down_ref = refs[count : count + 3]
        outs = refs[count + 3 : 2 * count + 3]
        x_ref, g_ref, u_ref, d_ref, xs_ref, y_ref, x_sem, w_sem, o_sem = refs[2 * count + 3 :]
        o_ref = x_ref
        xcopies = [
            pltpu.make_async_copy(
                block_refs[i], x_ref.at[pl.ds(starts[i], sizes[i])], x_sem.at[i]
            )
            for i in range(count)
        ]
        wcopies = []
        for e in range(local):
            wcopies.append(
                [
                    pltpu.make_async_copy(src.at[e], dst.at[e], w_sem.at[e, k])
                    for k, (src, dst) in enumerate(
                        [(gate_ref, g_ref), (up_ref, u_ref), (down_ref, d_ref)]
                    )
                ]
            )
        for copy in xcopies:
            copy.start()
        for trio in wcopies:
            for copy in trio:
                copy.start()
        for copy in xcopies:
            copy.wait()

        at = lax.broadcasted_iota(jnp.int32, (per, span), 0)

        def picks(g):
            return [
                slots_ref[e : e + 1, g * span : (g + 1) * span] == at for e in range(local)
            ]

        for g in range(groups):
            chosen = jnp.concatenate([p.astype(F32) for p in picks(g)], 0).astype(BF)
            picked = jnp.dot(
                chosen, x_ref[g * span : (g + 1) * span, :], preferred_element_type=F32
            ).astype(BF)
            for e in range(local):
                xs_ref[e, g * per : (g + 1) * per, :] = picked[e * per : (e + 1) * per]
        for e in range(local):
            for copy in wcopies[e]:
                copy.wait()
            rows = xs_ref[e]
            gate_part = jnp.dot(rows, g_ref[e], preferred_element_type=F32)
            up_part = jnp.dot(rows, u_ref[e], preferred_element_type=F32)
            inner = (gate_part / (1.0 + jnp.exp(-gate_part)) * up_part).astype(BF)
            result = jnp.dot(inner, d_ref[e], preferred_element_type=F32)
            for g in range(groups):
                chosen = slots_ref[e : e + 1, g * span : (g + 1) * span] == at
                share = jnp.sum(
                    jnp.where(chosen, shares_ref[e : e + 1, g * span : (g + 1) * span], 0.0),
                    axis=1,
                    keepdims=True,
                )
                part = result[g * per : (g + 1) * per] * share
                y_ref[g, e * per : (e + 1) * per, :] = part.astype(BF)
        ocopies = [
            pltpu.make_async_copy(
                o_ref.at[pl.ds(starts[i], sizes[i])], outs[i], o_sem.at[i]
            )
            for i in range(count)
        ]
        done = 0
        for g in range(groups):
            chosen = jnp.concatenate([p.astype(F32) for p in picks(g)], 0).astype(BF)
            o_ref[g * span : (g + 1) * span, :] = lax.dot_general(
                chosen, y_ref[g], (((0,), (0,)), ((), ())), preferred_element_type=F32
            ).astype(BF)
            while done < count and starts[done + 1] <= (g + 1) * span:
                ocopies[done].start()
                done += 1
        for copy in ocopies:
            copy.wait()

    vm = pl.BlockSpec(memory_space=pltpu.VMEM)
    return pl.pallas_call(
        kernel,
        name="experts",
        out_shape=[jax.ShapeDtypeStruct(b.shape, BF) for b in blocks],
        in_specs=[vm, vm] + [ANY] * (count + 3),
        out_specs=[ANY] * count,
        scratch_shapes=[
            pltpu.VMEM((tokens, width), BF),
            pltpu.VMEM(gate.shape, BF),
            pltpu.VMEM(up.shape, BF),
            pltpu.VMEM(down.shape, BF),
            pltpu.VMEM((local, groups * per, width), BF),
            pltpu.VMEM((groups, local * per, width), BF),
            pltpu.SemaphoreType.DMA((count,)),
            pltpu.SemaphoreType.DMA((local, 3)),
            pltpu.SemaphoreType.DMA((count,)),
        ],
        compiler_params=pltpu.CompilerParams(vmem_limit_bytes=VMEM_LIMIT),
        cost_estimate=pl.CostEstimate(
            flops=6 * local * groups * per * width * hidden,
            transcendentals=local * groups * per * hidden,
            bytes_accessed=6 * local * width * hidden + 4 * tokens * width,
        ),
    )(slots, shares, *blocks, gate, up, down)


def slot_tables(ids, shares, first, local, capacity, per_group):
    tokens = ids.shape[1]
    expert = (first + jnp.arange(local)).astype(ids.dtype)
    hit = ids[None] == expert[:, None, None]
    share = jnp.sum(jnp.where(hit, shares[None], 0.0), axis=1)
    match = jnp.any(hit, axis=1)
    blocks = match.reshape(local * (tokens // BLOCK), BLOCK)
    before = jnp.asarray(np.triu(np.ones((BLOCK, BLOCK)), 1), BF)
    rank = jnp.dot(blocks.astype(BF), before, preferred_element_type=F32)
    rank = rank.astype(jnp.int32).reshape(local, tokens)
    place = (jnp.arange(tokens) // BLOCK % per_group) * capacity
    return jnp.where(match, rank + place[None], -1), share


def solution(mesh):
    groups = mesh.shape["groups"]
    devices = mesh.shape["tok"]
    cores = 2
    chips = devices // cores
    layer = max(1, 4 // groups)
    if chips % layer:
        layer = 1
    levels = chips // layer
    if layer == 2:
        order = [z * 2 for z in range(levels)] + [z * 2 + 1 for z in reversed(range(levels))]
    else:
        order = list(range(chips))
    position = [order.index(chip) for chip in range(chips)]
    reach = chips // 2

    def shift(step):
        pairs = []
        for at, chip in enumerate(order):
            for core in range(cores):
                pairs.append((chip * cores + core, order[(at + step) % chips] * cores + core))
        return pairs

    forward, backward = shift(1), shift(-1)
    swap = [(i, i ^ 1) for i in range(devices)]
    across = [(g, g ^ 1) for g in range(groups)]
    diagonal = [
        (g * devices + t, (g ^ 1) * devices + (t ^ 1))
        for g in range(groups)
        for t in range(devices)
    ]

    def to_forward(v):
        return lax.ppermute(v, "tok", forward)

    def to_backward(v):
        return lax.ppermute(v, "tok", backward)

    def to_sibling(v):
        return lax.ppermute(v, "tok", swap)

    def to_across(v):
        return lax.ppermute(v, "groups", across)

    def to_diagonal(v):
        return lax.ppermute(v, ("groups", "tok"), diagonal)

    def ring_gather(block):
        found = {0: block}
        ahead = back = block
        for step in range(1, reach):
            ahead = to_forward(ahead)
            back = to_backward(back)
            found[chips - step] = ahead
            found[step] = back
        middle = block.shape[0] // 2
        return found, to_forward(ahead[:middle]), to_backward(back[middle:])

    def ring_reduce(parts, low, high):
        ahead = to_forward(low)
        back = to_backward(high)
        middle = low.shape[0]
        for step in range(reach - 1, 0, -1):
            one, two = parts[step], parts[chips - step]
            if step == reach - 1:
                one = jnp.concatenate([add(one[:middle], ahead), one[middle:]], 0)
                two = jnp.concatenate([two[:middle], add(two[middle:], back)], 0)
            else:
                one, two = add(one, ahead), add(two, back)
            ahead, back = to_forward(one), to_backward(two)
        return ahead, back

    def add(*values):
        total = values[0].astype(F32)
        for value in values[1:]:
            total = total + value.astype(F32)
        return total.astype(BF)

    def body(
        queries,
        new_keys,
        new_values,
        cache_keys,
        cache_values,
        cache_lens,
        residual,
        out_weight,
        norm_gain,
        expert_ids,
        route_weights,
        gate_weight,
        up_weight,
        down_weight,
    ):
        rows, width = residual.shape
        local = gate_weight.shape[0]
        top = expert_ids.shape[1]
        capacity = max(2, BLOCK * top * 3 // (2 * local * devices))
        half_rows = out_weight.shape[0]
        cols = width // 4
        me = lax.axis_index("tok")
        core = me % cores
        quarter = (lax.axis_index("groups") % 2) * 2 + core
        mine = jnp.asarray(position, jnp.int32)[me // cores]

        meta = jnp.concatenate([expert_ids.T.astype(F32), route_weights.T], 0)
        metas = [meta] + [lax.ppermute(meta, "tok", shift(-s)) for s in range(1, chips)]
        meta = jnp.concatenate(metas, 1)
        meta = jnp.concatenate([meta, to_sibling(meta)], 1)
        per_group = 1
        while per_group * capacity % 16 or per_group * BLOCK < 256:
            per_group *= 2
        slots, shares = slot_tables(
            meta[:top].astype(jnp.int32), meta[top:], me * local, local, capacity, per_group
        )

        own = lax.dynamic_slice_in_dim(out_weight, quarter * cols, cols, 1)
        other = to_sibling(lax.dynamic_slice_in_dim(out_weight, (quarter ^ 1) * cols, cols, 1))
        wfound, wlow, whigh = ring_gather(jnp.concatenate([own, other], 0))

        pieces = [[], [], [], []]
        for kv in range(KVH):
            piece = attention_piece(
                cache_lens, queries, new_keys, new_values, cache_keys, cache_values, kv
            )
            far = to_across(piece)
            pieces[0].append(piece)
            pieces[1].append(to_sibling(piece))
            pieces[2].append(far)
            pieces[3].append(to_sibling(far))

        offsets = [0] + [v for s in range(1, reach) for v in (s, chips - s)]
        chip_at = jnp.asarray(order, jnp.int32)[
            (mine + jnp.asarray(offsets + [reach], jnp.int32)) % chips
        ]
        first = chip_at * (cores * half_rows)
        table = jnp.stack([first + core * half_rows, first + (1 - core) * half_rows], 1)
        products = project(
            table.reshape(-1).astype(jnp.int32),
            pieces,
            [wfound[o] for o in offsets],
            wlow,
            whigh,
            half_rows,
        )
        returned = [
            products[0],
            to_sibling(products[1]),
            to_across(products[2]),
            to_diagonal(products[3]),
        ]
        columns = (quarter ^ jnp.arange(4)).astype(jnp.int32) * cols
        mixed, normed = mix_norm(columns, residual, norm_gain, returned)

        found, low, high = ring_gather(normed)
        near = [found[o] for o in range(reach)] + [low, high]
        near += [found[o] for o in range(reach + 1, chips)]
        blocks = near + [to_sibling(v) for v in near]
        sums = experts(
            slots, shares, blocks, gate_weight, up_weight, down_weight, capacity
        )
        count = len(near)
        crossed = [to_sibling(v) for v in sums[count:]]
        joined = [add(a, b) for a, b in zip(sums[1:count], crossed[1:])]
        joined = [None] + joined
        parts = {}
        for o in range(1, reach):
            parts[o] = joined[o]
            parts[chips - o] = joined[count - o]
        ahead, back = ring_reduce(parts, joined[reach], joined[reach + 1])
        final = mixed + (
            sums[0].astype(F32)
            + crossed[0].astype(F32)
            + ahead.astype(F32)
            + back.astype(F32)
        )
        return final.astype(BF)

    placed = (
        P(("groups", "tok"), None),
        P(("groups", "tok"), None),
        P(("groups", "tok"), None),
        P(("groups", "tok"), None),
        P(("groups", "tok"), None),
        P(("groups", "tok")),
        P(("groups", "tok"), None),
        P("tok", None),
        P(),
        P(("groups", "tok"), None),
        P(("groups", "tok"), None),
        P("tok", None, None),
        P("tok", None, None),
        P("tok", None, None),
    )
    return jax.shard_map(
        body, mesh=mesh, in_specs=placed, out_specs=P(("groups", "tok"), None), check_vma=False
    )
```

time: 506 us -> 261 us (0.52)
  the two profiles are of different devices: /device:TPU:13 before, /device:TPU:0 now
where the time goes in v1:
time: 261 us; the launch traced here: 260 us
  waiting for transfers between devices  114 us (44%)
  Pallas kernels  69.1 us (26%)
  starting transfers between devices  51.1 us (20%)
  other arithmetic  12.1 us (5%)
  local copies, waits for them, and re-layouts  10.8 us (4%)
    ppermute x12, waiting for transfers between devices, to_forward(): return lax.ppermute(v, 'tok', forward)  56.4 us
    pallas_call x4, Pallas kernels, attention_piece(): pl.pallas_call(kernel, name='attend', out_shape=jax.ShapeDtypeStruct((row...  33.3 us
    pallas_call x1, Pallas kernels, experts(): pl.pallas_call(kernel, name='experts', out_shape=[jax.ShapeDtypeStruct(b....  25.7 us
    ppermute x7, waiting for transfers between devices, body(): lax.ppermute(meta, 'tok', shift(-s))  20.8 us
    ppermute x12, waiting for transfers between devices, to_backward(): return lax.ppermute(v, 'tok', backward)  20.8 us
    ppermute x12, starting transfers between devices, to_forward(): return lax.ppermute(v, 'tok', forward)  19.1 us
    ppermute x5, waiting for transfers between devices, to_across(): return lax.ppermute(v, 'groups', across)  12.6 us
    ppermute x7, starting transfers between devices, body(): lax.ppermute(meta, 'tok', shift(-s))  9.49 us
  transfers between devices with their start and end apart: 66, of which 26 were waited for; matrix products, arithmetic and copies ran while one was open for 7% of the time, Pallas kernels for 13%

profile of v1, /device:TPU:0, one launch (start us, length us, event | category | flops | bytes accessed | tf_op | source)
XLA Modules:
  0.0 259.9 jit_solution(13592931986794398833)
XLA Ops:
  2.8 3.0 %collective-permute-start.14 = (bf16[512,512]{1,0:T(8,128)(2,1)S(1)}, bf16[512,512]{1,0:T(8,128)(2,1)S(1)}, u32[]{:S(2)}, u32[]{:S(2)}) collective-permute-start(bf16[512,512]{1,0:T(8,128)(2,1)S(1)} %pad_maximum_fusion.refs_17_), channel_id=1, source_target_pairs={{0,4},{1,5},{4,8},{5,9},{8,12},{9,13},{12,14},{13,15},{14,10},{15,... | collective-permute-start | bytes 1572872 | tf_op jit(solution)/shard_map/ppermute | solution.py:377
  5.8 12.2 %collective-permute-done.14.refs_19_ = bf16[512,512]{1,0:T(8,128)(2,1)S(1)} collective-permute-done((bf16[512,512]{1,0:T(8,128)(2,1)S(1)}, bf16[512,512]{1,0:T(8,128)(2,1)S(1)}, u32[]{:S(2)}, u32[]{:S(2)}) %collective-permute-start.14) | collective-permute-done | bytes 524320 | tf_op jit(solution)/shard_map/ppermute | solution.py:377
  18.0 1.8 collective-permute-start.16
  20.7 8.3 %attend.6.refs_3_ = bf16[128,1024]{1,0:T(8,128)(2,1)} custom-call(s32[1]{0:T(128)S(6)} %copy.41.lens_ref, bf16[128,4096]{1,0:T(8,128)(2,1)} %q_ref.7, bf16[128,512]{1,0:T(8,128)(2,1)} %kn_ref.7, bf16[128,512]{1,0:T(8,128)(2,1)} %vn_ref.7, bf16[2048,512]{1,0:T(8,128)(2,1)} %kc_ref.7, bf16[2048,512]{1,0:T(8,128)(2,1)} %vc_ref.7), custom_call_target="tpu_custom_call" | custom-call | flops 2281701376 | bytes 1638400 | tf_op jit(solution)/shard_map/attend/pallas_call | solution.py:61
  33.4 8.3 %attend.7.refs_4_ = bf16[128,1024]{1,0:T(8,128)(2,1)} custom-call(s32[1]{0:T(128)S(6)} %copy.41.lens_ref, bf16[128,4096]{1,0:T(8,128)(2,1)} %q_ref.7, bf16[128,512]{1,0:T(8,128)(2,1)} %kn_ref.7, bf16[128,512]{1,0:T(8,128)(2,1)} %vn_ref.7, bf16[2048,512]{1,0:T(8,128)(2,1)} %kc_ref.7, bf16[2048,512]{1,0:T(8,128)(2,1)} %vc_ref.7), custom_call_target="tpu_custom_call" | custom-call | flops 2281701376 | bytes 1638400 | tf_op jit(solution)/shard_map/attend/pallas_call | solution.py:61
  43.3 8.4 %attend.5.refs_2_ = bf16[128,1024]{1,0:T(8,128)(2,1)} custom-call(s32[1]{0:T(128)S(6)} %copy.41.lens_ref, bf16[128,4096]{1,0:T(8,128)(2,1)} %q_ref.7, bf16[128,512]{1,0:T(8,128)(2,1)} %kn_ref.7, bf16[128,512]{1,0:T(8,128)(2,1)} %vn_ref.7, bf16[2048,512]{1,0:T(8,128)(2,1)} %kc_ref.7, bf16[2048,512]{1,0:T(8,128)(2,1)} %vc_ref.7), custom_call_target="tpu_custom_call" | custom-call | flops 2281701376 | bytes 1638400 | tf_op jit(solution)/shard_map/attend/pallas_call | solution.py:61
  52.4 8.3 %attend.4.refs_1_ = bf16[128,1024]{1,0:T(8,128)(2,1)} custom-call(s32[1]{0:T(128)S(6)} %copy.41.lens_ref, bf16[128,4096]{1,0:T(8,128)(2,1)} %q_ref.7, bf16[128,512]{1,0:T(8,128)(2,1)} %kn_ref.7, bf16[128,512]{1,0:T(8,128)(2,1)} %vn_ref.7, bf16[2048,512]{1,0:T(8,128)(2,1)} %kc_ref.7, bf16[2048,512]{1,0:T(8,128)(2,1)} %vc_ref.7), custom_call_target="tpu_custom_call" | custom-call | flops 2281701376 | bytes 1638400 | tf_op jit(solution)/shard_map/attend/pallas_call | solution.py:61
  66.4 3.8 %collective-permute-done.4.refs_9_ = bf16[128,1024]{1,0:T(8,128)(2,1)S(1)} collective-permute-done((bf16[128,1024]{1,0:T(8,128)(2,1)}, bf16[128,1024]{1,0:T(8,128)(2,1)S(1)}, u32[]{:S(2)}, u32[]{:S(2)}) %collective-permute-start.4) | collective-permute-done | bytes 262176 | tf_op jit(solution)/shard_map/ppermute | solution.py:386
  70.7 4.6 %collective-permute-done.5.refs_10_ = bf16[128,1024]{1,0:T(8,128)(2,1)} collective-permute-done((bf16[128,1024]{1,0:T(8,128)(2,1)S(1)}, bf16[128,1024]{1,0:T(8,128)(2,1)}, u32[]{:S(2)}, u32[]{:S(2)}) %collective-permute-start.5) | collective-permute-done | bytes 262176 | tf_op jit(solution)/shard_map/ppermute | solution.py:386
  78.2 6.1 %collective-permute-done.19.refs_24_ = bf16[256,512]{1,0:T(8,128)(2,1)S(1)} collective-permute-done((bf16[256,512]{1,0:T(8,128)(2,1)}, bf16[256,512]{1,0:T(8,128)(2,1)S(1)}, u32[]{:S(2)}, u32[]{:S(2)}) %collective-permute-start.19) | collective-permute-done | bytes 262176 | tf_op jit(solution)/shard_map/ppermute | solution.py:377
  86.3 7.6 %project.1 = (bf16[128,512]{1,0:T(8,128)(2,1)}, bf16[128,512]{1,0:T(8,128)(2,1)}, bf16[128,512]{1,0:T(8,128)(2,1)}, bf16[128,512]{1,0:T(8,128)(2,1)}) custom-call(s32[16]{0:T(128)} %reshape.67.refs_0_, bf16[128,1024]{1,0:T(8,128)(2,1)} %attend.4.refs_1_, bf16[128,1024]{1,0:T(8,128)(2,1)} %attend.5.refs_2_, bf16[128,1024]{1,0:T(8,128)(2,1)} %attend.6.refs_3_, ...), custom_call_target="tpu_custom_call" | custom-call | flops 2147483648 | bytes 8388608 | tf_op jit(solution)/shard_map/project/pallas_call | solution.py:157
  96.4 4.2 %collective-permute-done.22.refs_2_ = bf16[128,512]{1,0:T(8,128)(2,1)S(1)} collective-permute-done((bf16[128,512]{1,0:T(8,128)(2,1)}, bf16[128,512]{1,0:T(8,128)(2,1)S(1)}, u32[]{:S(2)}, u32[]{:S(2)}) %collective-permute-start.22) | collective-permute-done | bytes 131104 | tf_op jit(solution)/shard_map/ppermute | solution.py:386
  103.0 2.5 mixnorm.1
  107.6 2.6 collective-permute-start.29
  113.5 6.5 %collective-permute-done.35.refs_8_ = bf16[128,2048]{1,0:T(8,128)(2,1)S(1)} collective-permute-done((bf16[128,2048]{1,0:T(8,128)(2,1)}, bf16[128,2048]{1,0:T(8,128)(2,1)S(1)}, u32[]{:S(2)}, u32[]{:S(2)}) %collective-permute-start.35) | collective-permute-done | bytes 524320 | tf_op jit(solution)/shard_map/ppermute | solution.py:377
  122.6 10.1 %collective-permute-done.25 = f32[16,128]{1,0:T(8,128)S(1)} collective-permute-done((f32[16,128]{1,0:T(8,128)S(1)}, f32[16,128]{1,0:T(8,128)S(1)}, u32[]{:S(2)}, u32[]{:S(2)}) %collective-permute-start.25) | collective-permute-done | bytes 8224 | tf_op jit(solution)/shard_map/ppermute | solution.py:450
  132.7 5.5 %collective-permute-done.26 = f32[16,128]{1,0:T(8,128)S(1)} collective-permute-done((f32[16,128]{1,0:T(8,128)S(1)}, f32[16,128]{1,0:T(8,128)S(1)}, u32[]{:S(2)}, u32[]{:S(2)}) %collective-permute-start.26) | collective-permute-done | bytes 8224 | tf_op jit(solution)/shard_map/ppermute | solution.py:450
  138.2 2.7 %collective-permute-start.27 = (f32[16,128]{1,0:T(8,128)S(1)}, f32[16,128]{1,0:T(8,128)S(1)}, u32[]{:S(2)}, u32[]{:S(2)}) collective-permute-start(f32[16,128]{1,0:T(8,128)S(1)} %get-tuple-element.73), channel_id=1, source_target_pairs={{0,14},{1,15},{4,10},{5,11},{8,6},{9,7},{12,2},{13,3},{14,0},{15,1... | collective-permute-start | bytes 24584 | tf_op jit(solution)/shard_map/ppermute | solution.py:450
  140.9 3.6 %collective-permute-done.27 = f32[16,128]{1,0:T(8,128)S(1)} collective-permute-done((f32[16,128]{1,0:T(8,128)S(1)}, f32[16,128]{1,0:T(8,128)S(1)}, u32[]{:S(2)}, u32[]{:S(2)}) %collective-permute-start.27) | collective-permute-done | bytes 8224 | tf_op jit(solution)/shard_map/ppermute | solution.py:450
  144.5 2.0 collective-permute-start.33
  148.8 7.9 %collective-permute-done.33.refs_2_ = bf16[128,2048]{1,0:T(8,128)(2,1)S(1)} collective-permute-done((bf16[128,2048]{1,0:T(8,128)(2,1)S(1)}, bf16[128,2048]{1,0:T(8,128)(2,1)S(1)}, u32[]{:S(2)}, u32[]{:S(2)}) %collective-permute-start.33) | collective-permute-done | bytes 524320 | tf_op jit(solution)/shard_map/ppermute | solution.py:380
  156.7 2.0 collective-permute-start.34
  160.1 7.4 %collective-permute-done.34.refs_3_ = bf16[128,2048]{1,0:T(8,128)(2,1)S(1)} collective-permute-done((bf16[128,2048]{1,0:T(8,128)(2,1)S(1)}, bf16[128,2048]{1,0:T(8,128)(2,1)S(1)}, u32[]{:S(2)}, u32[]{:S(2)}) %collective-permute-start.34) | collective-permute-done | bytes 524320 | tf_op jit(solution)/shard_map/ppermute | solution.py:380
  168.6 2.0 collective-permute-start.39
  181.2 25.7 %experts.1 = (bf16[128,2048]{1,0:T(8,128)(2,1)}, bf16[128,2048]{1,0:T(8,128)(2,1)}, bf16[128,2048]{1,0:T(8,128)(2,1)}, bf16[128,2048]{1,0:T(8,128)(2,1)}, bf16[6...) custom-call(s32[4,2048]{1,0:T(4,128)} %add_select_fusion.slots_ref, ...), custom_call_target="tpu_custom_call" | custom-call | flops 7247757312 | bytes 35651584 | tf_op jit(solution)/shard_map/experts/pallas_call | solution.py:304
  210.2 2.1 collective-permute-start.54
  216.0 2.6 %collective-permute-done.54 = bf16[64,2048]{1,0:T(8,128)(2,1)S(1)} collective-permute-done((bf16[64,2048]{1,0:T(8,128)(2,1)S(1)}, bf16[64,2048]{1,0:T(8,128)(2,1)S(1)}, u32[]{:S(2)}, u32[]{:S(2)}) %collective-permute-start.54) | collective-permute-done | bytes 262176 | tf_op jit(solution)/shard_map/ppermute | solution.py:377
  218.7 2.1 collective-permute-start.55
  222.5 9.7 %collective-permute-done.55 = bf16[128,2048]{1,0:T(8,128)(2,1)S(1)} collective-permute-done((bf16[128,2048]{1,0:T(8,128)(2,1)S(1)}, bf16[128,2048]{1,0:T(8,128)(2,1)S(1)}, u32[]{:S(2)}, u32[]{:S(2)}) %collective-permute-start.55) | collective-permute-done | bytes 524320 | tf_op jit(solution)/shard_map/ppermute | solution.py:377
  232.4 1.8 collective-permute-start.56
  235.4 9.6 %collective-permute-done.56 = bf16[128,2048]{1,0:T(8,128)(2,1)S(1)} collective-permute-done((bf16[128,2048]{1,0:T(8,128)(2,1)S(1)}, bf16[128,2048]{1,0:T(8,128)(2,1)S(1)}, u32[]{:S(2)}, u32[]{:S(2)}) %collective-permute-start.56) | collective-permute-done | bytes 524320 | tf_op jit(solution)/shard_map/ppermute | solution.py:377
  248.0 9.1 %collective-permute-done.57 = bf16[128,2048]{1,0:T(8,128)(2,1)S(1)} collective-permute-done((bf16[128,2048]{1,0:T(8,128)(2,1)S(1)}, bf16[128,2048]{1,0:T(8,128)(2,1)S(1)}, u32[]{:S(2)}, u32[]{:S(2)}) %collective-permute-start.57) | collective-permute-done | bytes 524320 | tf_op jit(solution)/shard_map/ppermute | solution.py:377
  (245 shorter events, 64.5 us)
Async XLA Ops:
  2.8 15.2 %collective-permute-start.14 = (bf16[512,512]{1,0:T(8,128)(2,1)S(1)}, bf16[512,512]{1,0:T(8,128)(2,1)S(1)}, u32[]{:S(2)}, u32[]{:S(2)}) collective-permute-start(bf16[512,512]{1,0:T(8,128)(2,1)S(1)} %pad_maximum_fusion.refs_17_), channel_id=1, source_target_pairs={{0,4},{1,5},{4,8},{5,9},{8,12},{9,13},{12,14},{13,15},{14,10},{15,... | collective-permute-start | bytes 1572872 | tf_op jit(solution)/shard_map/ppermute | solution.py:377
  5.8 14.0 %collective-permute-start.13 = (bf16[512,512]{1,0:T(8,128)(2,1)S(1)}, bf16[512,512]{1,0:T(8,128)(2,1)S(1)}, u32[]{:S(2)}, u32[]{:S(2)}) collective-permute-start(bf16[512,512]{1,0:T(8,128)(2,1)S(1)} %pad_maximum_fusion.refs_17_), channel_id=1, source_target_pairs={{0,2},{1,3},{4,0},{5,1},{8,4},{9,5},{12,8},{13,9},{14,12},{15,13},... | collective-permute-start | bytes 1572872 | tf_op jit(solution)/shard_map/ppermute | solution.py:380
  18.0 13.4 %collective-permute-start.16 = (bf16[512,512]{1,0:T(8,128)(2,1)S(1)}, bf16[512,512]{1,0:T(8,128)(2,1)S(1)}, u32[]{:S(2)}, u32[]{:S(2)}) collective-permute-start(bf16[512,512]{1,0:T(8,128)(2,1)S(1)} %collective-permute-done.14.refs_19_), channel_id=1, source_target_pairs={{0,4},{1,5},{4,8},{5,9},{8,12},{9,13},{12,14},{13,15},{14,10},{15,... | collective-permute-start | bytes 1572872 | tf_op jit(solution)/shard_map/ppermute | solution.py:377
  19.8 13.1 %collective-permute-start.15 = (bf16[512,512]{1,0:T(8,128)(2,1)S(1)}, bf16[512,512]{1,0:T(8,128)(2,1)}, u32[]{:S(2)}, u32[]{:S(2)}) collective-permute-start(bf16[512,512]{1,0:T(8,128)(2,1)S(1)} %collective-permute-done.13.refs_18_), channel_id=1, source_target_pairs={{0,2},{1,3},{4,0},{5,1},{8,4},{9,5},{12,8},{13,9},{14,12},{15,13},... | collective-permute-start | bytes 1572872 | tf_op jit(solution)/shard_map/ppermute | solution.py:380
  29.0 14.3 %collective-permute-start.6 = (bf16[128,1024]{1,0:T(8,128)(2,1)}, bf16[128,1024]{1,0:T(8,128)(2,1)S(1)}, u32[]{:S(2)}, u32[]{:S(2)}) collective-permute-start(bf16[128,1024]{1,0:T(8,128)(2,1)} %attend.6.refs_3_), channel_id=1, source_target_pairs={{0,16},{16,0},{1,17},{17,1},{2,18},{18,2},{3,19},{19,3},{4,20},{20... | collective-permute-start | bytes 786440 | tf_op jit(solution)/shard_map/ppermute | solution.py:386
  30.7 30.0 %collective-permute-start.2 = (bf16[128,1024]{1,0:T(8,128)(2,1)}, bf16[128,1024]{1,0:T(8,128)(2,1)S(1)}, u32[]{:S(2)}, u32[]{:S(2)}) collective-permute-start(bf16[128,1024]{1,0:T(8,128)(2,1)} %attend.6.refs_3_), channel_id=1, source_target_pairs={{0,1},{1,0},{2,3},{3,2},{4,5},{5,4},{6,7},{7,6},{8,9},{9,8},{10,11... | collective-permute-start | bytes 786440 | tf_op jit(solution)/shard_map/ppermute | solution.py:383
  31.4 31.6 %collective-permute-start.18 = (bf16[512,512]{1,0:T(8,128)(2,1)S(1)}, bf16[512,512]{1,0:T(8,128)(2,1)S(1)}, u32[]{:S(2)}, u32[]{:S(2)}) collective-permute-start(bf16[512,512]{1,0:T(8,128)(2,1)S(1)} %collective-permute-done.16.refs_21_), channel_id=1, source_target_pairs={{0,4},{1,5},{4,8},{5,9},{8,12},{9,13},{12,14},{13,15},{14,10},{15,... | collective-permute-start | bytes 1572872 | tf_op jit(solution)/shard_map/ppermute | solution.py:377
  32.9 30.2 %collective-permute-start.17 = (bf16[512,512]{1,0:T(8,128)(2,1)}, bf16[512,512]{1,0:T(8,128)(2,1)S(1)}, u32[]{:S(2)}, u32[]{:S(2)}) collective-permute-start(bf16[512,512]{1,0:T(8,128)(2,1)} %collective-permute-done.15.refs_20_), channel_id=1, source_target_pairs={{0,2},{1,3},{4,0},{5,1},{8,4},{9,5},{12,8},{13,9},{14,12},{15,13},... | collective-permute-start | bytes 1572872 | tf_op jit(solution)/shard_map/ppermute | solution.py:380
  41.8 19.6 %collective-permute-start.7 = (bf16[128,1024]{1,0:T(8,128)(2,1)}, bf16[128,1024]{1,0:T(8,128)(2,1)S(1)}, u32[]{:S(2)}, u32[]{:S(2)}) collective-permute-start(bf16[128,1024]{1,0:T(8,128)(2,1)} %attend.7.refs_4_), channel_id=1, source_target_pairs={{0,16},{16,0},{1,17},{17,1},{2,18},{18,2},{3,19},{19,3},{4,20},{20... | collective-permute-start | bytes 786440 | tf_op jit(solution)/shard_map/ppermute | solution.py:386
  43.3 18.2 %collective-permute-start.3 = (bf16[128,1024]{1,0:T(8,128)(2,1)}, bf16[128,1024]{1,0:T(8,128)(2,1)S(1)}, u32[]{:S(2)}, u32[]{:S(2)}) collective-permute-start(bf16[128,1024]{1,0:T(8,128)(2,1)} %attend.7.refs_4_), channel_id=1, source_target_pairs={{0,1},{1,0},{2,3},{3,2},{4,5},{5,4},{6,7},{7,6},{8,9},{9,8},{10,11... | collective-permute-start | bytes 786440 | tf_op jit(solution)/shard_map/ppermute | solution.py:383
  61.5 13.8 %collective-permute-start.5 = (bf16[128,1024]{1,0:T(8,128)(2,1)S(1)}, bf16[128,1024]{1,0:T(8,128)(2,1)}, u32[]{:S(2)}, u32[]{:S(2)}) collective-permute-start(bf16[128,1024]{1,0:T(8,128)(2,1)S(1)} %copy-done.26), channel_id=1, source_target_pairs={{0,16},{16,0},{1,17},{17,1},{2,18},{18,2},{3,19},{19,3},{4,20},{20... | collective-permute-start | bytes 786440 | tf_op jit(solution)/shard_map/ppermute | solution.py:386
  63.0 12.3 %collective-permute-start.1 = (bf16[128,1024]{1,0:T(8,128)(2,1)S(1)}, bf16[128,1024]{1,0:T(8,128)(2,1)S(1)}, u32[]{:S(2)}, u32[]{:S(2)}) collective-permute-start(bf16[128,1024]{1,0:T(8,128)(2,1)S(1)} %copy-done.26), channel_id=1, source_target_pairs={{0,1},{1,0},{2,3},{3,2},{4,5},{5,4},{6,7},{7,6},{8,9},{9,8},{10,11... | collective-permute-start | bytes 786440 | tf_op jit(solution)/shard_map/ppermute | solution.py:383
  63.1 13.8 %collective-permute-start.10 = (bf16[128,1024]{1,0:T(8,128)(2,1)S(1)}, bf16[128,1024]{1,0:T(8,128)(2,1)S(1)}, u32[]{:S(2)}, u32[]{:S(2)}) collective-permute-start(bf16[128,1024]{1,0:T(8,128)(2,1)S(1)} %collective-permute-done.6.refs_11_), channel_id=1, source_target_pairs={{0,1},{1,0},{2,3},{3,2},{4,5},{5,4},{6,7},{7,6},{8,9},{9,8},{10,11... | collective-permute-start | bytes 786440 | tf_op jit(solution)/shard_map/ppermute | solution.py:383
  105.6 14.5 %collective-permute-start.35 = (bf16[128,2048]{1,0:T(8,128)(2,1)}, bf16[128,2048]{1,0:T(8,128)(2,1)S(1)}, u32[]{:S(2)}, u32[]{:S(2)}) collective-permute-start(bf16[128,2048]{1,0:T(8,128)(2,1)} %get-tuple-element.34.refs_0_), channel_id=1, source_target_pairs={{0,4},{1,5},{4,8},{5,9},{8,12},{9,13},{12,14},{13,15},{14,10},{15,... | collective-permute-start | bytes 1572872 | tf_op jit(solution)/shard_map/ppermute | solution.py:377
  107.1 37.4 %collective-permute-start.32 = (bf16[128,2048]{1,0:T(8,128)(2,1)}, bf16[128,2048]{1,0:T(8,128)(2,1)S(1)}, u32[]{:S(2)}, u32[]{:S(2)}) collective-permute-start(bf16[128,2048]{1,0:T(8,128)(2,1)} %get-tuple-element.34.refs_0_), channel_id=1, source_target_pairs={{0,2},{1,3},{4,0},{5,1},{8,4},{9,5},{12,8},{13,9},{14,12},{15,13},... | collective-permute-start | bytes 1572872 | tf_op jit(solution)/shard_map/ppermute | solution.py:380
  107.6 39.1 %collective-permute-start.29 = (f32[16,128]{1,0:T(8,128)S(1)}, f32[16,128]{1,0:T(8,128)S(1)}, u32[]{:S(2)}, u32[]{:S(2)}) collective-permute-start(f32[16,128]{1,0:T(8,128)S(1)} %get-tuple-element.73), channel_id=1, source_target_pairs={{0,8},{1,9},{4,12},{5,13},{8,14},{9,15},{12,10},{13,11},{14,6},{15... | collective-permute-start | bytes 24584 | tf_op jit(solution)/shard_map/ppermute | solution.py:450
  110.2 36.5 %collective-permute-start.28 = (f32[16,128]{1,0:T(8,128)S(1)}, f32[16,128]{1,0:T(8,128)S(1)}, u32[]{:S(2)}, u32[]{:S(2)}) collective-permute-start(f32[16,128]{1,0:T(8,128)S(1)} %get-tuple-element.73), channel_id=1, source_target_pairs={{0,12},{1,13},{4,14},{5,15},{8,10},{9,11},{12,6},{13,7},{14,2},{15... | collective-permute-start | bytes 24584 | tf_op jit(solution)/shard_map/ppermute | solution.py:450
  120.1 26.5 %collective-permute-start.36 = (bf16[128,2048]{1,0:T(8,128)(2,1)S(1)}, bf16[128,2048]{1,0:T(8,128)(2,1)S(1)}, u32[]{:S(2)}, u32[]{:S(2)}) collective-permute-start(bf16[128,2048]{1,0:T(8,128)(2,1)S(1)} %collective-permute-done.35.refs_8_), channel_id=1, source_target_pairs={{0,4},{1,5},{4,8},{5,9},{8,12},{9,13},{12,14},{13,15},{14,10},{15,... | collective-permute-start | bytes 1572872 | tf_op jit(solution)/shard_map/ppermute | solution.py:377
  146.6 12.7 %collective-permute-start.37 = (bf16[128,2048]{1,0:T(8,128)(2,1)S(1)}, bf16[128,2048]{1,0:T(8,128)(2,1)S(1)}, u32[]{:S(2)}, u32[]{:S(2)}) collective-permute-start(bf16[128,2048]{1,0:T(8,128)(2,1)S(1)} %collective-permute-done.36.refs_7_), channel_id=1, source_target_pairs={{0,4},{1,5},{4,8},{5,9},{8,12},{9,13},{12,14},{13,15},{14,10},{15,... | collective-permute-start | bytes 1572872 | tf_op jit(solution)/shard_map/ppermute | solution.py:377
  148.3 20.3 %collective-permute-start.40 = (bf16[128,2048]{1,0:T(8,128)(2,1)}, bf16[128,2048]{1,0:T(8,128)(2,1)}, u32[]{:S(2)}, u32[]{:S(2)}) collective-permute-start(bf16[128,2048]{1,0:T(8,128)(2,1)} %get-tuple-element.34.refs_0_), channel_id=1, source_target_pairs={{0,1},{1,0},{2,3},{3,2},{4,5},{5,4},{6,7},{7,6},{8,9},{9,8},{10,11... | collective-permute-start | bytes 1572872 | tf_op jit(solution)/shard_map/ppermute | solution.py:383
  158.7 15.4 %collective-permute-start.48 = (bf16[128,2048]{1,0:T(8,128)(2,1)S(1)}, bf16[128,2048]{1,0:T(8,128)(2,1)}, u32[]{:S(2)}, u32[]{:S(2)}) collective-permute-start(bf16[128,2048]{1,0:T(8,128)(2,1)S(1)} %collective-permute-done.35.refs_8_), channel_id=1, source_target_pairs={{0,1},{1,0},{2,3},{3,2},{4,5},{5,4},{6,7},{7,6},{8,9},{9,8},{10,11... | collective-permute-start | bytes 1572872 | tf_op jit(solution)/shard_map/ppermute | solution.py:383
  158.7 15.3 %collective-permute-start.41 = (bf16[128,2048]{1,0:T(8,128)(2,1)S(1)}, bf16[128,2048]{1,0:T(8,128)(2,1)}, u32[]{:S(2)}, u32[]{:S(2)}) collective-permute-start(bf16[128,2048]{1,0:T(8,128)(2,1)S(1)} %collective-permute-done.32.refs_1_), channel_id=1, source_target_pairs={{0,1},{1,0},{2,3},{3,2},{4,5},{5,4},{6,7},{7,6},{8,9},{9,8},{10,11... | collective-permute-start | bytes 1572872 | tf_op jit(solution)/shard_map/ppermute | solution.py:383
  159.2 15.3 %collective-permute-start.47 = (bf16[128,2048]{1,0:T(8,128)(2,1)S(1)}, bf16[128,2048]{1,0:T(8,128)(2,1)}, u32[]{:S(2)}, u32[]{:S(2)}) collective-permute-start(bf16[128,2048]{1,0:T(8,128)(2,1)S(1)} %collective-permute-done.36.refs_7_), channel_id=1, source_target_pairs={{0,1},{1,0},{2,3},{3,2},{4,5},{5,4},{6,7},{7,6},{8,9},{9,8},{10,11... | collective-permute-start | bytes 1572872 | tf_op jit(solution)/shard_map/ppermute | solution.py:383
  207.5 14.5 %collective-permute-start.51 = (bf16[128,2048]{1,0:T(8,128)(2,1)}, bf16[128,2048]{1,0:T(8,128)(2,1)S(1)}, u32[]{:S(2)}, u32[]{:S(2)}) collective-permute-start(bf16[128,2048]{1,0:T(8,128)(2,1)} %get-tuple-element.40), channel_id=1, source_target_pairs={{0,1},{1,0},{2,3},{3,2},{4,5},{5,4},{6,7},{7,6},{8,9},{9,8},{10,11... | collective-permute-start | bytes 1572872 | tf_op jit(solution)/shard_map/ppermute | solution.py:383
  208.0 26.2 %collective-permute-start.59 = (bf16[128,2048]{1,0:T(8,128)(2,1)}, bf16[128,2048]{1,0:T(8,128)(2,1)S(1)}, u32[]{:S(2)}, u32[]{:S(2)}) collective-permute-start(bf16[128,2048]{1,0:T(8,128)(2,1)} %get-tuple-element.48), channel_id=1, source_target_pairs={{0,1},{1,0},{2,3},{3,2},{4,5},{5,4},{6,7},{7,6},{8,9},{9,8},{10,11... | collective-permute-start | bytes 1572872 | tf_op jit(solution)/shard_map/ppermute | solution.py:383
  218.7 13.5 %collective-permute-start.55 = (bf16[128,2048]{1,0:T(8,128)(2,1)S(1)}, bf16[128,2048]{1,0:T(8,128)(2,1)S(1)}, u32[]{:S(2)}, u32[]{:S(2)}) collective-permute-start(bf16[128,2048]{1,0:T(8,128)(2,1)S(1)} %pad_maximum_fusion.1), channel_id=1, source_target_pairs={{0,4},{1,5},{4,8},{5,9},{8,12},{9,13},{12,14},{13,15},{14,10},{15,... | collective-permute-start | bytes 1572872 | tf_op jit(solution)/shard_map/ppermute | solution.py:377
  221.8 13.0 %collective-permute-start.63 = (bf16[128,2048]{1,0:T(8,128)(2,1)S(1)}, bf16[128,2048]{1,0:T(8,128)(2,1)S(1)}, u32[]{:S(2)}, u32[]{:S(2)}) collective-permute-start(bf16[128,2048]{1,0:T(8,128)(2,1)S(1)} %pad_maximum_fusion.2), channel_id=1, source_target_pairs={{0,2},{1,3},{4,0},{5,1},{8,4},{9,5},{12,8},{13,9},{14,12},{15,13},... | collective-permute-start | bytes 1572872 | tf_op jit(solution)/shard_map/ppermute | solution.py:380
  222.0 13.4 %collective-permute-start.50 = (bf16[128,2048]{1,0:T(8,128)(2,1)S(1)}, bf16[128,2048]{1,0:T(8,128)(2,1)S(1)}, u32[]{:S(2)}, u32[]{:S(2)}) collective-permute-start(bf16[128,2048]{1,0:T(8,128)(2,1)S(1)} %copy-done.41), channel_id=1, source_target_pairs={{0,1},{1,0},{2,3},{3,2},{4,5},{5,4},{6,7},{7,6},{8,9},{9,8},{10,11... | collective-permute-start | bytes 1572872 | tf_op jit(solution)/shard_map/ppermute | solution.py:383
  222.0 24.8 %collective-permute-start.58 = (bf16[128,2048]{1,0:T(8,128)(2,1)S(1)}, bf16[128,2048]{1,0:T(8,128)(2,1)S(1)}, u32[]{:S(2)}, u32[]{:S(2)}) collective-permute-start(bf16[128,2048]{1,0:T(8,128)(2,1)S(1)} %copy-done.40), channel_id=1, source_target_pairs={{0,1},{1,0},{2,3},{3,2},{4,5},{5,4},{6,7},{7,6},{8,9},{9,8},{10,11... | collective-permute-start | bytes 1572872 | tf_op jit(solution)/shard_map/ppermute | solution.py:383
  232.4 12.6 %collective-permute-start.56 = (bf16[128,2048]{1,0:T(8,128)(2,1)S(1)}, bf16[128,2048]{1,0:T(8,128)(2,1)S(1)}, u32[]{:S(2)}, u32[]{:S(2)}) collective-permute-start(bf16[128,2048]{1,0:T(8,128)(2,1)S(1)} %add_convert_fusion.7), channel_id=1, source_target_pairs={{0,4},{1,5},{4,8},{5,9},{8,12},{9,13},{12,14},{13,15},{14,10},{15,... | collective-permute-start | bytes 1572872 | tf_op jit(solution)/shard_map/ppermute | solution.py:377
  235.0 12.1 %collective-permute-start.64 = (bf16[128,2048]{1,0:T(8,128)(2,1)S(1)}, bf16[128,2048]{1,0:T(8,128)(2,1)S(1)}, u32[]{:S(2)}, u32[]{:S(2)}) collective-permute-start(bf16[128,2048]{1,0:T(8,128)(2,1)S(1)} %add_convert_fusion.2), channel_id=1, source_target_pairs={{0,2},{1,3},{4,0},{5,1},{8,4},{9,5},{12,8},{13,9},{14,12},{15,13},... | collective-permute-start | bytes 1572872 | tf_op jit(solution)/shard_map/ppermute | solution.py:380
  235.4 12.6 %collective-permute-start.49 = (bf16[128,2048]{1,0:T(8,128)(2,1)S(1)}, bf16[128,2048]{1,0:T(8,128)(2,1)S(1)}, u32[]{:S(2)}, u32[]{:S(2)}) collective-permute-start(bf16[128,2048]{1,0:T(8,128)(2,1)S(1)} %copy-done.39), channel_id=1, source_target_pairs={{0,1},{1,0},{2,3},{3,2},{4,5},{5,4},{6,7},{7,6},{8,9},{9,8},{10,11... | collective-permute-start | bytes 1572872 | tf_op jit(solution)/shard_map/ppermute | solution.py:383
  (78 other events, 1133.8 us)
